TPU v7x, 32 devices: a whole 2x2x4 slice. The times are simulated.
32 devices in a mesh: dp: 8 (over y, x, core), space: 4 (over z).
Axes of the slice: x: 2, y: 2, z: 4, core: 2. Of those that a mesh axis runs over, the one named last changes fastest.
Arguments:
- volume: bfloat16 [8, 8, 8, 8, 512], P('dp', 'space'), may hold values from -6 to 6
- conv_one: bfloat16 [3, 3, 3, 512, 256], P(None, None, None, 'dp'), may hold values from -0.125 to 0.125
- mix_one: bfloat16 [256, 256], P('dp'), may hold values from -0.375 to 0.375
- conv_two: bfloat16 [3, 3, 3, 256, 128], P(None, None, None, 'dp'), may hold values from -0.1875 to 0.1875
- mix_two: bfloat16 [128, 128], P('dp'), may hold values from -0.5 to 0.5
Outputs:
- decoded: bfloat16 [8, 32, 32, 32, 128], P('dp', 'space')
All inputs are finite; a program needn't handle non-finite values.
Results may differ from a plain program's by a relative error of at most 0.007.
Values may be sent and summed in bfloat16 or wider, within the bound.
A program may use at most 64 MiB of HBM per device.

v0:
```python
import jax
import jax.numpy as jnp
from jax import lax
from jax.sharding import PartitionSpec as P

PHASE_TAPS = (((1, 0),), ((2, 0), (0, 1)))


def shifted(block, axis, distance):
    devices = range(lax.axis_size(axis))
    route = [(i - distance, i) for i in devices if i - distance in devices]
    return lax.ppermute(block, axis, route)


def phase_sum(padded, weight, planes, height, breadth, depth_taps):
    chans_in = padded.shape[-1]
    chans_out = weight.shape[-1]
    groups = []
    for taps_depth in depth_taps:
        for taps_rows in PHASE_TAPS:
            for taps_cols in PHASE_TAPS:
                total = None
                for depth_tap, depth_shift in taps_depth:
                    for row_tap, row_shift in taps_rows:
                        for col_tap, col_shift in taps_cols:
                            piece = padded[
                                depth_shift : depth_shift + planes,
                                row_shift : row_shift + height,
                                col_shift : col_shift + breadth,
                            ]
                            term = jnp.dot(
                                piece.reshape(-1, chans_in),
                                weight[depth_tap, row_tap, col_tap],
                                preferred_element_type=jnp.float32,
                            )
                            total = term if total is None else total + term
                groups.append(total)
    return jnp.stack(groups).reshape(len(depth_taps), 2, 2, planes, height, breadth, chans_out)


def alternate(phased):
    planes, height, breadth, chans = phased.shape[3:]
    return jnp.transpose(phased, (3, 0, 4, 1, 5, 2, 6)).reshape(
        2 * planes, 2 * height, 2 * breadth, chans
    )


def expand(field, weight, first):
    planes, height, breadth, chans = field.shape
    if first:
        plane = shifted(field[0:1], "space", -1)
    else:
        plane = shifted(field[0:1], "space", -1)
    padded = jnp.pad(jnp.concatenate([field, plane], 0), ((0, 0), (0, 1), (0, 1), (0, 0)))
    phased = phase_sum(padded, weight, planes, height, breadth, PHASE_TAPS)
    return alternate(phased)


def finish(conv, mixing):
    act = jax.nn.silu(conv).astype(jnp.bfloat16)
    mixed = jnp.dot(act.reshape(-1, act.shape[-1]), mixing, preferred_element_type=jnp.float32)
    return mixed.astype(jnp.bfloat16).reshape(conv.shape[:-1] + (mixing.shape[1],))


def per_device(volume, conv_one, mix_one, conv_two, mix_two):
    field = volume[0]
    kernel_one, mixing_one = (
        lax.all_gather(conv_one, "dp", axis=3, tiled=True),
        lax.all_gather(mix_one, "dp", axis=0, tiled=True),
    )
    upper = finish(expand(field, kernel_one, True), mixing_one)
    kernel_two, mixing_two = (
        lax.all_gather(conv_two, "dp", axis=3, tiled=True),
        lax.all_gather(mix_two, "dp", axis=0, tiled=True),
    )
    decoded = finish(expand(upper, kernel_two, False), mixing_two)
    return decoded[None]


def solution(mesh):
    return jax.shard_map(
        per_device,
        mesh=mesh,
        in_specs=(
            P("dp", "space", None, None, None),
            P(None, None, None, "dp", None),
            P("dp", None),
            P(None, None, None, "dp", None),
            P("dp", None),
        ),
        out_specs=P("dp", "space", None, None, None),
        check_vma=False,
    )
```

profile of v0, /device:TPU:0, one launch (start us, length us, event | category | flops | bytes accessed | tf_op | source)
XLA Modules:
  0.0 114.8 jit_solution(14823665278782194715)
XLA Ops:
  6.5 0.7 all-gather.3.cloned.1.call-update
  7.3 0.8 slice_bitcast_fusion.108
  8.2 1.3 %collective-permute-start = (bf16[1,8,8,512]{3,2,1,0:T(8,128)(2,1)S(1)}, bf16[1,8,8,512]{3,2,1,0:T(8,128)(2,1)S(1)}, u32[]{:S(2)}, u32[]{:S(2)}) collective-permute-start(bf16[1,8,8,512]{3,2,1,0:T(8,128)(2,1)S(1)} %slice_bitcast_fusion.108), channel_id=1, source_target_pairs={{1,0},{2,1},{3,2},{5,4},{6,5},{7,6},{9,8},{10,9},{11,10},{13,12},{... | collective-permute-start | bytes 196616 | tf_op jit(solution)/shard_map/ppermute | solution.py:12
  9.5 10.7 %all_gather.15 = bf16[128,128]{1,0:T(8,128)(2,1)S(1)} all-gather(bf16[16,128]{1,0:T(8,128)(2,1)} %param.9), channel_id=1, replica_groups=mesh['dp'=8,'space'=4] {'dp'}, dimensions={0}, use_global_device_ids=true | all-gather | bytes 36864 | tf_op jit(solution)/shard_map/all_gather | solution.py:74
  20.1 9.4 %all_gather.13 = bf16[256,256]{1,0:T(8,128)(2,1)S(1)} all-gather(bf16[32,256]{1,0:T(8,128)(2,1)} %param.7), channel_id=1, replica_groups=mesh['dp'=8,'space'=4] {'dp'}, dimensions={0}, use_global_device_ids=true | all-gather | bytes 147456 | tf_op jit(solution)/shard_map/all_gather | solution.py:69
  29.5 0.9 pad_maximum_fusion.1
  30.5 0.9 fusion.38
  31.3 30.0 %all-gather.3.cloned.1.call-done = bf16[3,3,3,512,256]{4,3,2,1,0:T(8,128)(2,1)} async-done(((bf16[3,3,3,64,256]{4,3,2,1,0:T(8,128)(2,1)}), bf16[3,3,3,512,256]{4,3,2,1,0:T(8,128)(2,1)}) %all-gather.3.cloned.1.call-update) | async-done | bytes 7077904 | tf_op jit(solution)/shard_map/all_gather | solution.py:68
  61.4 1.3 %fusion.29 = f32[8,128,256]{2,1,0:T(8,128)S(1)} fusion(bf16[128,512]{1,0:T(8,128)(2,1)} %bitcast.315, bf16[3,3,3,512,256]{4,3,2,1,0:T(8,128)(2,1)} %all-gather.3.cloned.1.call-done), kind=kOutput, calls=%fused_computation.78 | convolution fusion | flops 33554432 | bytes 524288 | tf_op jit(solution)/shard_map/dot_general | solution.py:31
  62.7 1.5 %fusion.37 = f32[128,256]{1,0:T(8,128)S(1)} fusion(bf16[128,512]{1,0:T(8,128)(2,1)} %bitcast.316, bf16[3,3,3,512,256]{4,3,2,1,0:T(8,128)(2,1)} %all-gather.3.cloned.1.call-done), kind=kOutput, calls=%fused_computation.123 | convolution fusion | flops 33554432 | bytes 524288 | tf_op jit(solution)/shard_map/dot_general | solution.py:31
  64.2 1.1 fusion.36
  65.4 1.1 fusion.35
  66.5 1.1 fusion.33
  67.7 1.1 fusion.32
  68.8 1.1 fusion.31
  70.0 1.1 convolution_add_fusion.35
  71.1 1.1 convolution_add_fusion.31
  72.3 1.1 convolution_add_fusion.34
  73.4 1.1 convolution_add_fusion.28
  74.6 1.1 convolution_add_fusion.30
  75.7 1.1 convolution_add_fusion.27
  79.6 0.8 copy.9
  80.5 0.7 reshape.55
  81.2 0.4 convolution_convert_fusion.1
  81.6 1.5 %collective-permute-start.1 = (bf16[1,16,16,256]{3,2,1,0:T(8,128)(2,1)S(1)}, bf16[1,16,16,256]{3,2,1,0:T(8,128)(2,1)S(1)}, u32[]{:S(2)}, u32[]{:S(2)}) collective-permute-start(bf16[1,16,16,256]{3,2,1,0:T(8,128)(2,1)S(1)} %bitcast.365), channel_id=1, source_target_pairs={{1,0},{2,1},{3,2},{5,4},{6,5},{7,6},{9,8},{10,9},{11,10},{13,12},{... | collective-permute-start | bytes 393224 | tf_op jit(solution)/shard_map/ppermute | solution.py:12
  83.1 7.0 %all-gather.5.cloned.1.call-done = bf16[3,3,3,256,128]{4,3,2,1,0:T(8,128)(2,1)} async-done(((bf16[3,3,3,32,128]{4,3,2,1,0:T(8,128)(2,1)}), bf16[3,3,3,256,128]{4,3,2,1,0:T(8,128)(2,1)}) %all-gather.5.cloned.1.call-update) | async-done | bytes 1769488 | tf_op jit(solution)/shard_map/all_gather | solution.py:73
  90.1 1.2 %fusion = f32[8,1024,128]{2,1,0:T(8,128)S(1)} fusion(bf16[1024,256]{1,0:T(8,128)(2,1)S(1)} %convolution_convert_fusion.1, bf16[3,3,3,256,128]{4,3,2,1,0:T(8,128)(2,1)} %all-gather.5.cloned.1.call-done), kind=kOutput, calls=%fused_computation.10 | convolution fusion | flops 67108864 | bytes 1114112 | tf_op jit(solution)/shard_map/dot_general | solution.py:31
  91.3 1.1 fusion.45
  92.5 1.1 fusion.44
  93.6 1.1 fusion.43
  96.0 0.3 pad_slice_fusion
  96.4 0.3 convolution_add_fusion.16
  96.7 0.3 convolution_add_fusion.12
  97.3 0.3 convolution_add_fusion.9
  97.6 0.3 convolution_add_fusion.11
  97.9 0.3 convolution_add_fusion.8
  98.2 0.3 convolution_add_fusion.6
  98.8 0.3 convolution_add_fusion.4
  99.1 0.3 convolution_add_fusion.3
  99.4 0.3 fusion.14
  99.7 0.3 fusion.12
  100.3 0.3 fusion.8
  100.7 0.3 convolution_add_fusion.2
  101.0 0.3 fusion.6
  101.3 0.3 convolution_add_fusion.1
  101.9 0.3 fusion.2
  102.2 3.3 %copy.7 = f32[2,2,2,4,16,16,128]{6,2,5,1,4,0,3:T(2,128)S(1)} copy(f32[2,2,2,4,16,16,128]{6,5,4,3,2,1,0:T(8,128)S(1)} %bitcast.335) | data formatting | bytes 8388608 | tf_op jit(solution)/shard_map/reshape | solution.py:38
  105.5 2.5 %convolution_convert_fusion = bf16[8192,128]{1,0:T(8,128)(2,1)} fusion(bf16[128,128]{1,0:T(8,128)(2,1)S(1)} %all_gather.15, f32[8192,128]{1,0:T(8,128)S(1)} %bitcast.342), kind=kOutput, calls=%fused_computation | convolution fusion | flops 274726912 | bytes 6324224 | tf_op jit(solution)/shard_map/dot_general | solution.py:61
  (37 shorter events, 5.3 us)
Async XLA Ops:
  6.5 57.7 %copy-start = (bf16[1,2,8,8,512]{4,3,2,1,0:T(8,128)(2,1)S(1)}, bf16[1,2,8,8,512]{4,3,2,1,0:T(8,128)(2,1)}, u32[]{:S(2)}) copy-start(bf16[1,2,8,8,512]{4,3,2,1,0:T(8,128)(2,1)} %param.5) | copy-start | bytes 393220
  6.5 54.8 %all-gather.3.cloned.1.call-start = ((), (), s32[]{:S(2)}) async-start(), calls=%async_computation | async-start | bytes 7962624 | tf_op jit(solution)/shard_map/all_gather | solution.py:68
  7.3 82.8 %all-gather.5.cloned.1.call-start = ((), (), s32[]{:S(2)}) async-start(), calls=%async_computation.1 | async-start | bytes 1990656 | tf_op jit(solution)/shard_map/all_gather | solution.py:73
  8.2 21.3 %collective-permute-start = (bf16[1,8,8,512]{3,2,1,0:T(8,128)(2,1)S(1)}, bf16[1,8,8,512]{3,2,1,0:T(8,128)(2,1)S(1)}, u32[]{:S(2)}, u32[]{:S(2)}) collective-permute-start(bf16[1,8,8,512]{3,2,1,0:T(8,128)(2,1)S(1)} %slice_bitcast_fusion.108), channel_id=1, source_target_pairs={{1,0},{2,1},{3,2},{5,4},{6,5},{7,6},{9,8},{10,9},{11,10},{13,12},{... | collective-permute-start | bytes 196616 | tf_op jit(solution)/shard_map/ppermute | solution.py:12
  61.4 15.5 %copy-start.1 = (bf16[3,3,3,512,256]{4,3,2,1,0:T(8,128)(2,1)S(1)}, bf16[3,3,3,512,256]{4,3,2,1,0:T(8,128)(2,1)}, u32[]{:S(2)}) copy-start(bf16[3,3,3,512,256]{4,3,2,1,0:T(8,128)(2,1)} %all-gather.3.cloned.1.call-done) | copy-start | bytes 21233668
  81.6 14.3 %collective-permute-start.1 = (bf16[1,16,16,256]{3,2,1,0:T(8,128)(2,1)S(1)}, bf16[1,16,16,256]{3,2,1,0:T(8,128)(2,1)S(1)}, u32[]{:S(2)}, u32[]{:S(2)}) collective-permute-start(bf16[1,16,16,256]{3,2,1,0:T(8,128)(2,1)S(1)} %bitcast.365), channel_id=1, source_target_pairs={{1,0},{2,1},{3,2},{5,4},{6,5},{7,6},{9,8},{10,9},{11,10},{13,12},{... | collective-permute-start | bytes 393224 | tf_op jit(solution)/shard_map/ppermute | solution.py:12
  90.1 4.7 %copy-start.2 = (bf16[3,3,3,256,128]{4,3,2,1,0:T(8,128)(2,1)S(1)}, bf16[3,3,3,256,128]{4,3,2,1,0:T(8,128)(2,1)}, u32[]{:S(2)}) copy-start(bf16[3,3,3,256,128]{4,3,2,1,0:T(8,128)(2,1)} %all-gather.5.cloned.1.call-done) | copy-start | bytes 5308420
Sparse Core Ops, SparseCore 0:
  9.3 52.0 all-gather.2
  63.2 26.7 all-gather.4
where the time goes:
time: 116 us; the launch traced here: 115 us
  waiting for transfers between devices  37.7 us (33%)
  matrix products  32.5 us (28%)
  blocking collectives  20 us (17%)
  between operations  13.8 us (12%)
  local copies, waits for them, and re-layouts  6.06 us (5%)
  starting transfers between devices  2.79 us (2%)
  other arithmetic  1.89 us (2%)
    all_gather x1, waiting for transfers between devices, per_device(): lax.all_gather(conv_one, 'dp', axis=3, tiled=True)  30 us
    dot_general x54, matrix products, phase_sum(): jnp.dot(piece.reshape(-1, chans_in), weight[depth_tap, row_tap, col_tap],...  29.6 us
    all_gather x1, blocking collectives, per_device(): lax.all_gather(mix_two, 'dp', axis=0, tiled=True)  10.7 us
    all_gather x1, blocking collectives, per_device(): lax.all_gather(mix_one, 'dp', axis=0, tiled=True)  9.36 us
    all_gather x1, waiting for transfers between devices, per_device(): lax.all_gather(conv_two, 'dp', axis=3, tiled=True)  6.95 us
    reshape x2, local copies, waits for them, and re-layouts, phase_sum(): jnp.stack(groups)  4.09 us
    dot_general x2, matrix products, finish(): jnp.dot(act.reshape(-1, act.shape[-1]), mixing, preferred_element_type=jn...  2.96 us
    ppermute x2, starting transfers between devices, shifted(): return lax.ppermute(block, axis, route)  2.75 us
  transfers between devices with their start and end apart: 4, of which 2 were waited for; matrix products, arithmetic and copies ran while one was open for 25% of the time, Pallas kernels for 0%

commit v1 on v0

--- a/solution.py
+++ b/solution.py
@@ -4,6 +4,32 @@
 from jax.sharding import PartitionSpec as P
 
 PHASE_TAPS = (((1, 0),), ((2, 0), (0, 1)))
+
+
+def links_touch(mat, d0):
+    back = list(mat.shape[1:])
+    back[d0] *= mat.shape[0]
+    current_block = jnp.moveaxis(mat, 0, d0).reshape(back)
+    return current_block
+
+
+def _try_all_circles(block_here, axis_tag, k_dim):
+    n_lanes = lax.axis_size(axis_tag)
+    gallery = [(at, (at + 1) % n_lanes) for at in range(n_lanes)]
+    top, w_next = ([], [])
+    found = [(kk, jj) for jj, kk in gallery]
+    for idx in tuple(range(n_lanes - 1)):
+        if idx % 2 == 0:
+            top.append(lax.ppermute(top[-1] if top else block_here, axis_tag, perm=gallery))
+        else:
+            w_next.append(
+                lax.ppermute(w_next[-1] if w_next else block_here, axis_name=axis_tag, perm=found)
+            )
+    everything = jnp.stack([*top[::-1], block_here, *w_next], 0)
+    moved = lax.axis_index(axis_tag) - len(top)
+    everything = everything[(jnp.arange(n_lanes) - moved) % n_lanes]
+    x_next = links_touch(everything, k_dim)
+    return x_next
 
 
 def shifted(block, axis, distance):
@@ -66,7 +92,7 @@
     field = volume[0]
     kernel_one, mixing_one = (
         lax.all_gather(conv_one, "dp", axis=3, tiled=True),
-        lax.all_gather(mix_one, "dp", axis=0, tiled=True),
+        _try_all_circles(mix_one, "dp", 0),
     )
     upper = finish(expand(field, kernel_one, True), mixing_one)
     kernel_two, mixing_two = (

time: 116 us -> 115 us (level)
  blocking collectives: 20 us -> 10 us
  starting transfers between devices: 2.79 us -> 10.3 us
  waiting for transfers between devices: 37.7 us -> 39.1 us
    all_gather x1 -> x0, blocking collectives: 9.36 us -> none  [per_device(): lax.all_gather(mix_one, 'dp', axis=0, tiled=True)]
    ppermute x0 -> x7, starting transfers between devices: none -> 7.53 us  [the longest x3 7.01 us: _try_all_circles(): lax.ppermute(w_next[-1] if w_next else block_here, axis_name=axis_tag, pe...]
    ppermute x0 -> x7, waiting for transfers between devices: none -> 4.82 us  [the longest x4 4.81 us: _try_all_circles(): lax.ppermute(top[-1] if top else block_here, axis_tag, perm=gallery)]
    all_gather x1, waiting for transfers between devices: 30 us -> 26 us  [per_device(): lax.all_gather(conv_one, 'dp', axis=3, tiled=True)]
    reshape x2 -> x1, local copies, waits for them, and re-layouts: 4.09 us -> 3.28 us  [phase_sum(): jnp.stack(groups)]
  transfers between devices with their start and end apart: 4 -> 11, of which waited for: 2 -> 5; matrix products, arithmetic and copies ran while one was open for 25% -> 25% of each run, Pallas kernels for 0% -> 0%
where the time goes in v1:
time: 115 us
  waiting for transfers between devices  39.1 us (34%)
  matrix products  32.4 us (28%)
  between operations  13.9 us (12%)
  starting transfers between devices  10.3 us (9%)
  blocking collectives  10 us (9%)
  local copies, waits for them, and re-layouts  6.56 us (6%)
  other arithmetic  2.2 us (2%)
    dot_general x54, matrix products, phase_sum(): jnp.dot(piece.reshape(-1, chans_in), weight[depth_tap, row_tap, col_tap],...  29.6 us
    all_gather x1, waiting for transfers between devices, per_device(): lax.all_gather(conv_one, 'dp', axis=3, tiled=True)  26 us
    all_gather x1, blocking collectives, per_device(): lax.all_gather(mix_two, 'dp', axis=0, tiled=True)  10 us
    all_gather x1, waiting for transfers between devices, per_device(): lax.all_gather(conv_two, 'dp', axis=3, tiled=True)  7.58 us
    ppermute x3, starting transfers between devices, _try_all_circles(): lax.ppermute(w_next[-1] if w_next else block_here, axis_name=axis_tag, pe...  7.01 us
    ppermute x4, waiting for transfers between devices, _try_all_circles(): lax.ppermute(top[-1] if top else block_here, axis_tag, perm=gallery)  4.81 us
    reshape x1, local copies, waits for them, and re-layouts, phase_sum(): jnp.stack(groups)  3.28 us
    dot_general x2, matrix products, finish(): jnp.dot(act.reshape(-1, act.shape[-1]), mixing, preferred_element_type=jn...  2.83 us
  transfers between devices with their start and end apart: 11, of which 5 were waited for; matrix products, arithmetic and copies ran while one was open for 25% of the time, Pallas kernels for 0%

profile of v1, /device:TPU:0, one launch (start us, length us, event | category | flops | bytes accessed | tf_op | source)
XLA Modules:
  0.0 114.6 jit_solution(9186889178884043747)
XLA Ops:
  6.5 0.7 all-gather.3.cloned.1.call-update
  7.3 0.5 collective-permute-start.1
  7.8 2.9 %collective-permute-start.5 = (bf16[32,256]{1,0:T(8,128)(2,1)}, bf16[32,256]{1,0:T(8,128)(2,1)S(1)}, u32[]{:S(2)}, u32[]{:S(2)}) collective-permute-start(bf16[32,256]{1,0:T(8,128)(2,1)} %param.7), channel_id=1, source_target_pairs={{4,0},{8,4},{12,8},{16,12},{20,16},{24,20},{28,24},{0,28},{5,1},{9... | collective-permute-start | bytes 49160 | tf_op jit(solution)/shard_map/ppermute | solution.py:26
  10.8 1.6 %collective-permute-done.1 = bf16[32,256]{1,0:T(8,128)(2,1)S(1)} collective-permute-done((bf16[32,256]{1,0:T(8,128)(2,1)}, bf16[32,256]{1,0:T(8,128)(2,1)S(1)}, u32[]{:S(2)}, u32[]{:S(2)}) %collective-permute-start.1) | collective-permute-done | bytes 16416 | tf_op jit(solution)/shard_map/ppermute | solution.py:23
  12.3 0.8 slice_bitcast_fusion.108
  13.2 1.3 %collective-permute-start = (bf16[1,8,8,512]{3,2,1,0:T(8,128)(2,1)S(1)}, bf16[1,8,8,512]{3,2,1,0:T(8,128)(2,1)S(1)}, u32[]{:S(2)}, u32[]{:S(2)}) collective-permute-start(bf16[1,8,8,512]{3,2,1,0:T(8,128)(2,1)S(1)} %slice_bitcast_fusion.108), channel_id=1, source_target_pairs={{1,0},{2,1},{3,2},{5,4},{6,5},{7,6},{9,8},{10,9},{11,10},{13,12},{... | collective-permute-start | bytes 196616 | tf_op jit(solution)/shard_map/ppermute | solution.py:38
  14.5 1.9 %collective-permute-done.2 = bf16[32,256]{1,0:T(8,128)(2,1)S(1)} collective-permute-done((bf16[32,256]{1,0:T(8,128)(2,1)S(1)}, bf16[32,256]{1,0:T(8,128)(2,1)S(1)}, u32[]{:S(2)}, u32[]{:S(2)}) %collective-permute-start.2) | collective-permute-done | bytes 16416 | tf_op jit(solution)/shard_map/ppermute | solution.py:23
  16.4 2.7 %collective-permute-start.6 = (bf16[32,256]{1,0:T(8,128)(2,1)S(1)}, bf16[32,256]{1,0:T(8,128)(2,1)S(1)}, u32[]{:S(2)}, u32[]{:S(2)}) collective-permute-start(bf16[32,256]{1,0:T(8,128)(2,1)S(1)} %collective-permute-done.5), channel_id=1, source_target_pairs={{4,0},{8,4},{12,8},{16,12},{20,16},{24,20},{28,24},{0,28},{5,1},{9... | collective-permute-start | bytes 49160 | tf_op jit(solution)/shard_map/ppermute | solution.py:26
  19.1 1.3 %collective-permute-done.3 = bf16[32,256]{1,0:T(8,128)(2,1)S(1)} collective-permute-done((bf16[32,256]{1,0:T(8,128)(2,1)S(1)}, bf16[32,256]{1,0:T(8,128)(2,1)S(1)}, u32[]{:S(2)}, u32[]{:S(2)}) %collective-permute-start.3) | collective-permute-done | bytes 16416 | tf_op jit(solution)/shard_map/ppermute | solution.py:23
  20.5 10.0 %all_gather.11 = bf16[128,128]{1,0:T(8,128)(2,1)S(1)} all-gather(bf16[16,128]{1,0:T(8,128)(2,1)} %param.9), channel_id=1, replica_groups=mesh['dp'=8,'space'=4] {'dp'}, dimensions={0}, use_global_device_ids=true | all-gather | bytes 36864 | tf_op jit(solution)/shard_map/all_gather | solution.py:100
  30.5 1.4 %collective-permute-start.7 = (bf16[32,256]{1,0:T(8,128)(2,1)S(1)}, bf16[32,256]{1,0:T(8,128)(2,1)S(1)}, u32[]{:S(2)}, u32[]{:S(2)}) collective-permute-start(bf16[32,256]{1,0:T(8,128)(2,1)S(1)} %collective-permute-done.6), channel_id=1, source_target_pairs={{4,0},{8,4},{12,8},{16,12},{20,16},{24,20},{28,24},{0,28},{5,1},{9... | collective-permute-start | bytes 49160 | tf_op jit(solution)/shard_map/ppermute | solution.py:26
  31.9 0.7 constant_dynamic-update-slice_fusion.3
  32.7 0.9 pad_maximum_fusion.1
  33.7 0.6 gather_fusion
  34.2 0.9 fusion.42
  35.1 26.0 %all-gather.3.cloned.1.call-done = bf16[3,3,3,512,256]{4,3,2,1,0:T(8,128)(2,1)} async-done(((bf16[3,3,3,64,256]{4,3,2,1,0:T(8,128)(2,1)}), bf16[3,3,3,512,256]{4,3,2,1,0:T(8,128)(2,1)}) %all-gather.3.cloned.1.call-update) | async-done | bytes 7077904 | tf_op jit(solution)/shard_map/all_gather | solution.py:94
  61.1 1.4 %fusion.29 = f32[8,128,256]{2,1,0:T(8,128)S(1)} fusion(bf16[128,512]{1,0:T(8,128)(2,1)} %bitcast.345, bf16[3,3,3,512,256]{4,3,2,1,0:T(8,128)(2,1)} %all-gather.3.cloned.1.call-done), kind=kOutput, calls=%fused_computation.79 | convolution fusion | flops 33554432 | bytes 524288 | tf_op jit(solution)/shard_map/dot_general | solution.py:57
  62.5 1.5 %fusion.41 = f32[128,256]{1,0:T(8,128)S(1)} fusion(bf16[128,512]{1,0:T(8,128)(2,1)} %bitcast.346, bf16[3,3,3,512,256]{4,3,2,1,0:T(8,128)(2,1)} %all-gather.3.cloned.1.call-done), kind=kOutput, calls=%fused_computation.128 | convolution fusion | flops 33554432 | bytes 524288 | tf_op jit(solution)/shard_map/dot_general | solution.py:57
  64.0 1.1 fusion.40
  65.1 1.1 fusion.39
  66.3 1.1 fusion.37
  67.4 1.1 fusion.36
  68.6 1.1 %fusion.35 = f32[128,256]{1,0:T(8,128)S(1)} fusion(bf16[128,512]{1,0:T(8,128)(2,1)S(1)} %bitcast.351, bf16[3,3,3,512,256]{4,3,2,1,0:T(8,128)(2,1)} %all-gather.3.cloned.1.call-done), kind=kOutput, calls=%fused_computation.104 | convolution fusion | flops 33554432 | bytes 524288 | tf_op jit(solution)/shard_map/dot_general | solution.py:57
  69.7 1.1 %convolution_add_fusion.35 = f32[128,256]{1,0:T(8,128)S(1)} fusion(f32[128,256]{1,0:T(8,128)S(1)} %fusion.39, bf16[128,512]{1,0:T(8,128)(2,1)S(1)} %bitcast.377, bf16[3,3,3,512,256]{4,3,2,1,0:T(8,128)(2,1)} %all-gather.3.cloned.1.call-done), kind=kOutput, calls=%fused_computation.71 | convolution fusion | flops 33587200 | bytes 655360 | tf_op jit(solution)/shard_map/dot_general | solution.py:57
  70.9 1.1 convolution_add_fusion.31
  72.0 1.1 convolution_add_fusion.34
  73.2 1.1 convolution_add_fusion.28
  74.3 1.1 convolution_add_fusion.30
  75.5 1.1 convolution_add_fusion.27
  79.7 0.5 copy.11
  80.7 1.5 %collective-permute-start.8 = (bf16[1,16,16,256]{3,2,1,0:T(8,128)(2,1)S(1)}, bf16[1,16,16,256]{3,2,1,0:T(8,128)(2,1)S(1)}, u32[]{:S(2)}, u32[]{:S(2)}) collective-permute-start(bf16[1,16,16,256]{3,2,1,0:T(8,128)(2,1)S(1)} %bitcast.395), channel_id=1, source_target_pairs={{1,0},{2,1},{3,2},{5,4},{6,5},{7,6},{9,8},{10,9},{11,10},{13,12},{... | collective-permute-start | bytes 393224 | tf_op jit(solution)/shard_map/ppermute | solution.py:38
  82.2 7.6 %all-gather.5.cloned.1.call-done = bf16[3,3,3,256,128]{4,3,2,1,0:T(8,128)(2,1)} async-done(((bf16[3,3,3,32,128]{4,3,2,1,0:T(8,128)(2,1)}), bf16[3,3,3,256,128]{4,3,2,1,0:T(8,128)(2,1)}) %all-gather.5.cloned.1.call-update) | async-done | bytes 1769488 | tf_op jit(solution)/shard_map/all_gather | solution.py:99
  89.8 1.2 %fusion = f32[8,1024,128]{2,1,0:T(8,128)S(1)} fusion(bf16[1024,256]{1,0:T(8,128)(2,1)S(1)} %convolution_convert_fusion.1, bf16[3,3,3,256,128]{4,3,2,1,0:T(8,128)(2,1)} %all-gather.5.cloned.1.call-done), kind=kOutput, calls=%fused_computation.11 | convolution fusion | flops 67108864 | bytes 1114112 | tf_op jit(solution)/shard_map/dot_general | solution.py:57
  91.1 1.1 fusion.49
  92.2 1.1 fusion.48
  93.3 1.1 fusion.47
  95.8 0.3 pad_slice_fusion
  96.4 0.3 convolution_add_fusion.12
  97.4 0.3 convolution_add_fusion.11
  97.7 0.3 convolution_add_fusion.8
  98.0 0.3 convolution_add_fusion.6
  98.9 0.3 convolution_add_fusion.3
  99.2 0.3 fusion.14
  99.5 0.3 fusion.12
  100.7 0.3 fusion.6
  101.0 0.3 convolution_add_fusion.1
  101.9 3.3 %copy.12 = f32[2,2,2,4,16,16,128]{6,2,5,1,4,0,3:T(2,128)S(1)} copy(f32[2,2,2,4,16,16,128]{6,5,4,3,2,1,0:T(8,128)S(1)} %bitcast.365) | data formatting | bytes 8388608 | tf_op jit(solution)/shard_map/reshape | solution.py:64
  105.2 2.5 %convolution_convert_fusion = bf16[8192,128]{1,0:T(8,128)(2,1)} fusion(bf16[128,128]{1,0:T(8,128)(2,1)S(1)} %all_gather.11, f32[8192,128]{1,0:T(8,128)S(1)} %bitcast.372), kind=kOutput, calls=%fused_computation.1 | convolution fusion | flops 274726912 | bytes 6324224 | tf_op jit(solution)/shard_map/dot_general | solution.py:87
  (62 shorter events, 7.9 us)
Async XLA Ops:
  6.5 57.4 %copy-start = (bf16[1,2,8,8,512]{4,3,2,1,0:T(8,128)(2,1)S(1)}, bf16[1,2,8,8,512]{4,3,2,1,0:T(8,128)(2,1)}, u32[]{:S(2)}) copy-start(bf16[1,2,8,8,512]{4,3,2,1,0:T(8,128)(2,1)} %param.5) | copy-start | bytes 393220
  6.5 54.6 %all-gather.3.cloned.1.call-start = ((), (), s32[]{:S(2)}) async-start(), calls=%async_computation | async-start | bytes 7962624 | tf_op jit(solution)/shard_map/all_gather | solution.py:94
  7.3 82.5 %all-gather.5.cloned.1.call-start = ((), (), s32[]{:S(2)}) async-start(), calls=%async_computation.1 | async-start | bytes 1990656 | tf_op jit(solution)/shard_map/all_gather | solution.py:99
  7.3 5.0 %collective-permute-start.1 = (bf16[32,256]{1,0:T(8,128)(2,1)}, bf16[32,256]{1,0:T(8,128)(2,1)S(1)}, u32[]{:S(2)}, u32[]{:S(2)}) collective-permute-start(bf16[32,256]{1,0:T(8,128)(2,1)} %param.7), channel_id=1, source_target_pairs={{0,4},{4,8},{8,12},{12,16},{16,20},{20,24},{24,28},{28,0},{1,5},{5... | collective-permute-start | bytes 49160 | tf_op jit(solution)/shard_map/ppermute | solution.py:23
  7.8 8.6 %collective-permute-start.5 = (bf16[32,256]{1,0:T(8,128)(2,1)}, bf16[32,256]{1,0:T(8,128)(2,1)S(1)}, u32[]{:S(2)}, u32[]{:S(2)}) collective-permute-start(bf16[32,256]{1,0:T(8,128)(2,1)} %param.7), channel_id=1, source_target_pairs={{4,0},{8,4},{12,8},{16,12},{20,16},{24,20},{28,24},{0,28},{5,1},{9... | collective-permute-start | bytes 49160 | tf_op jit(solution)/shard_map/ppermute | solution.py:26
  12.3 4.1 %collective-permute-start.2 = (bf16[32,256]{1,0:T(8,128)(2,1)S(1)}, bf16[32,256]{1,0:T(8,128)(2,1)S(1)}, u32[]{:S(2)}, u32[]{:S(2)}) collective-permute-start(bf16[32,256]{1,0:T(8,128)(2,1)S(1)} %collective-permute-done.1), channel_id=1, source_target_pairs={{0,4},{4,8},{8,12},{12,16},{16,20},{20,24},{24,28},{28,0},{1,5},{5... | collective-permute-start | bytes 49160 | tf_op jit(solution)/shard_map/ppermute | solution.py:23
  13.2 19.5 %collective-permute-start = (bf16[1,8,8,512]{3,2,1,0:T(8,128)(2,1)S(1)}, bf16[1,8,8,512]{3,2,1,0:T(8,128)(2,1)S(1)}, u32[]{:S(2)}, u32[]{:S(2)}) collective-permute-start(bf16[1,8,8,512]{3,2,1,0:T(8,128)(2,1)S(1)} %slice_bitcast_fusion.108), channel_id=1, source_target_pairs={{1,0},{2,1},{3,2},{5,4},{6,5},{7,6},{9,8},{10,9},{11,10},{13,12},{... | collective-permute-start | bytes 196616 | tf_op jit(solution)/shard_map/ppermute | solution.py:38
  16.4 4.1 %collective-permute-start.3 = (bf16[32,256]{1,0:T(8,128)(2,1)S(1)}, bf16[32,256]{1,0:T(8,128)(2,1)S(1)}, u32[]{:S(2)}, u32[]{:S(2)}) collective-permute-start(bf16[32,256]{1,0:T(8,128)(2,1)S(1)} %collective-permute-done.2), channel_id=1, source_target_pairs={{0,4},{4,8},{8,12},{12,16},{16,20},{20,24},{24,28},{28,0},{1,5},{5... | collective-permute-start | bytes 49160 | tf_op jit(solution)/shard_map/ppermute | solution.py:23
  16.4 14.1 %collective-permute-start.6 = (bf16[32,256]{1,0:T(8,128)(2,1)S(1)}, bf16[32,256]{1,0:T(8,128)(2,1)S(1)}, u32[]{:S(2)}, u32[]{:S(2)}) collective-permute-start(bf16[32,256]{1,0:T(8,128)(2,1)S(1)} %collective-permute-done.5), channel_id=1, source_target_pairs={{4,0},{8,4},{12,8},{16,12},{20,16},{24,20},{28,24},{0,28},{5,1},{9... | collective-permute-start | bytes 49160 | tf_op jit(solution)/shard_map/ppermute | solution.py:26
  20.5 11.4 %collective-permute-start.4 = (bf16[32,256]{1,0:T(8,128)(2,1)S(1)}, bf16[32,256]{1,0:T(8,128)(2,1)S(1)}, u32[]{:S(2)}, u32[]{:S(2)}) collective-permute-start(bf16[32,256]{1,0:T(8,128)(2,1)S(1)} %collective-permute-done.3), channel_id=1, source_target_pairs={{0,4},{4,8},{8,12},{12,16},{16,20},{20,24},{24,28},{28,0},{1,5},{5... | collective-permute-start | bytes 49160 | tf_op jit(solution)/shard_map/ppermute | solution.py:23
  30.5 3.1 %collective-permute-start.7 = (bf16[32,256]{1,0:T(8,128)(2,1)S(1)}, bf16[32,256]{1,0:T(8,128)(2,1)S(1)}, u32[]{:S(2)}, u32[]{:S(2)}) collective-permute-start(bf16[32,256]{1,0:T(8,128)(2,1)S(1)} %collective-permute-done.6), channel_id=1, source_target_pairs={{4,0},{8,4},{12,8},{16,12},{20,16},{24,20},{28,24},{0,28},{5,1},{9... | collective-permute-start | bytes 49160 | tf_op jit(solution)/shard_map/ppermute | solution.py:26
  61.1 15.5 %copy-start.1 = (bf16[3,3,3,512,256]{4,3,2,1,0:T(8,128)(2,1)S(1)}, bf16[3,3,3,512,256]{4,3,2,1,0:T(8,128)(2,1)}, u32[]{:S(2)}) copy-start(bf16[3,3,3,512,256]{4,3,2,1,0:T(8,128)(2,1)} %all-gather.3.cloned.1.call-done) | copy-start | bytes 21233668
  80.7 14.9 %collective-permute-start.8 = (bf16[1,16,16,256]{3,2,1,0:T(8,128)(2,1)S(1)}, bf16[1,16,16,256]{3,2,1,0:T(8,128)(2,1)S(1)}, u32[]{:S(2)}, u32[]{:S(2)}) collective-permute-start(bf16[1,16,16,256]{3,2,1,0:T(8,128)(2,1)S(1)} %bitcast.395), channel_id=1, source_target_pairs={{1,0},{2,1},{3,2},{5,4},{6,5},{7,6},{9,8},{10,9},{11,10},{13,12},{... | collective-permute-start | bytes 393224 | tf_op jit(solution)/shard_map/ppermute | solution.py:38
  89.8 4.7 %copy-start.2 = (bf16[3,3,3,256,128]{4,3,2,1,0:T(8,128)(2,1)S(1)}, bf16[3,3,3,256,128]{4,3,2,1,0:T(8,128)(2,1)}, u32[]{:S(2)}) copy-start(bf16[3,3,3,256,128]{4,3,2,1,0:T(8,128)(2,1)} %all-gather.5.cloned.1.call-done) | copy-start | bytes 5308420
Sparse Core Ops, SparseCore 0:
  9.3 51.7 all-gather.2
  63.0 26.7 all-gather.4
